TPU v7x, 32 devices: a whole 2x2x4 slice. The times are simulated.
32 devices in a mesh: groups: 2 (over x), space: 16 (over z, y, core).
Axes of the slice: x: 2, y: 2, z: 4, core: 2. Of those that a mesh axis runs over, the one named last changes fastest.
Arguments:
- eigvecs: bfloat16 [32, 64, 2, 3, 128], P('groups', 'space'), parts along dimension 0, may hold values from -1.3515625 to 1.3515625
- phase_index: int32 [128], P('groups'), parts along dimension 0, may hold values from 0 to 47
- perambulator: bfloat16 [512, 2, 128, 128], P(('groups', 'space')), parts along dimension 0, may hold values from -0.046875 to 0.046875
- tile_sink: int32 [512, 1], P(('groups', 'space')), parts along dimension 0, may hold values from 0 to 15; in each aligned block of 16 rows (0 to 15, 16 to 31, ...) at most 2 rows name the same one
- tile_sep: int32 [512], P(('groups', 'space')), parts along dimension 0, may hold values from 0 to 7
- tile_diagram: int32 [512], P(('groups', 'space')), parts along dimension 0, may hold values from 0 to 1
Outputs:
- elementals: bfloat16 [32, 2, 128, 128], P(('groups', 'space')), parts along dimension 0
- correlator: float32 [512, 2], P(('groups', 'space')), parts along dimension 0
There are 2 independent parts, one for each index of `groups`. A program takes and returns all parts, laid end to end along the dimension named above; each array names one. Nothing has to cross between parts.
Inputs may be any that keep to these rules, and one draw needn't show every extreme that they name: `tile_sink`: in the tiles of one device no sink time is named by more than 2 tiles.
All inputs are finite; a program needn't handle non-finite values.
Results may differ from a plain program's by a relative error of at most 0.0048.
Values may be sent and summed in bfloat16 or wider, within the bound.
A program may use at most 128 MiB of HBM per device.

v0:
```python
import math

import jax
import jax.numpy as jnp
from jax import lax
from jax.sharding import PartitionSpec as P

PERIOD = 48


def make_right(vecs, cosine, sine):
    real_part = vecs[..., 0, :, :].astype(jnp.float32)
    imag_part = vecs[..., 1, :, :].astype(jnp.float32)
    cos_col = cosine[:, None, None]
    sin_col = sine[:, None, None]
    first = (cos_col * real_part - sin_col * imag_part).astype(jnp.bfloat16)
    second = (sin_col * real_part + cos_col * imag_part).astype(jnp.bfloat16)
    top = jnp.stack([first, second], -2)
    bottom = jnp.stack([second, -first], -2)
    return jnp.stack([top, bottom], -4)


def phases(indices):
    angle = 2.0 * math.pi / PERIOD * indices.astype(jnp.float32)
    return (jnp.cos(angle), jnp.sin(angle))


def contract_tiles(sink_mat, source_mat, tiles, diagram):

    def mult(left, right):
        return jnp.einsum("bij,bjk->bik", left, right, preferred_element_type=jnp.float32)

    tile_re = tiles[:, 0]
    tile_im = tiles[:, 1]
    trans_re = jnp.swapaxes(tile_re, 1, 2)
    trans_im = -jnp.swapaxes(tile_im, 1, 2)
    flag = (diagram == 1)[:, None, None]
    left_re = jnp.where(flag, trans_re, tile_re)
    left_im = jnp.where(flag, trans_im, tile_im)
    right_re = jnp.where(flag, tile_re, trans_re)
    right_im = jnp.where(flag, tile_im, trans_im)
    sink_re = sink_mat[:, 0]
    sink_im = sink_mat[:, 1]
    src_re = jnp.swapaxes(source_mat[:, 0], 1, 2)
    src_im = -jnp.swapaxes(source_mat[:, 1], 1, 2)
    first_re = mult(sink_re, left_re) - mult(sink_im, left_im)
    first_im = mult(sink_re, left_im) + mult(sink_im, left_re)
    second_re = jnp.swapaxes(mult(src_re, right_re) - mult(src_im, right_im), 1, 2)
    second_im = jnp.swapaxes(mult(src_re, right_im) + mult(src_im, right_re), 1, 2)
    trace_re = jnp.sum(first_re * second_re - first_im * second_im, axis=(1, 2))
    trace_im = jnp.sum(first_re * second_im + first_im * second_re, axis=(1, 2))
    return jnp.stack([trace_re, trace_im], -1)


def run_blocks(step_fn, items, total):
    block = math.gcd(32, total)
    shaped = tuple((item.reshape((total // block, block) + item.shape[1:]) for item in items))
    result = lax.map(step_fn, shaped)
    return result.reshape((total,) + result.shape[2:])


def local(eigvecs, phase_index, perambulator, tile_sink, tile_sep, tile_diagram):
    tile_count = perambulator.shape[0]
    sinks = tile_sink[:, 0]
    cosine, sine = phases(phase_index)
    slices = lax.all_to_all(eigvecs, "space", split_axis=0, concat_axis=1, tiled=True)
    vecs = slices[0]
    right = make_right(vecs, cosine, sine)
    value = jnp.einsum("spck,spcol->okl", vecs, right, preferred_element_type=jnp.float32)
    elemental = value.astype(jnp.bfloat16)[None]
    gathered = lax.all_gather(elemental, "space", axis=0, tiled=True)
    time_count = gathered.shape[0]
    sources = jnp.mod(sinks - tile_sep, time_count)

    def holder_block(items):
        tiles, sink_ids, source_ids, diagram = items
        return contract_tiles(gathered[sink_ids], gathered[source_ids], tiles, diagram)

    correlator = run_blocks(holder_block, (perambulator, sinks, sources, tile_diagram), tile_count)
    return (elemental, correlator)


def solution(mesh):
    return jax.shard_map(
        local,
        mesh=mesh,
        in_specs=(
            P("groups", "space", None, None, None),
            P("groups"),
            P(("groups", "space"), None, None, None),
            P(("groups", "space"), None),
            P(("groups", "space")),
            P(("groups", "space")),
        ),
        out_specs=(P(("groups", "space"), None, None, None), P(("groups", "space"), None)),
        check_vma=False,
    )
```

profile of v0, /device:TPU:1, one launch (start us, length us, event | category | flops | bytes accessed | tf_op | source)
XLA Modules:
  0.0 76.5 jit_solution(16801960626893713510)
XLA Ops:
  7.2 7.5 %all-to-all-start = ((bf16[16,4,2,3,128]{4,2,3,1,0:T(2,128)(2,1)}), bf16[16,4,2,3,128]{4,2,3,1,0:T(2,128)(2,1)S(1)}, u32[]{:S(2)}, u32[]{:S(2)}) async-start(bf16[16,4,2,3,128]{4,2,3,1,0:T(2,128)(2,1)} %param.6), calls=%async_computation | async-start | bytes 196608 | tf_op jit(solution)/shard_map/all_to_all | solution.py:66
  14.8 6.3 %all-to-all-done = bf16[16,4,2,3,128]{4,2,3,1,0:T(2,128)(2,1)S(1)} async-done(((bf16[16,4,2,3,128]{4,2,3,1,0:T(2,128)(2,1)}), bf16[16,4,2,3,128]{4,2,3,1,0:T(2,128)(2,1)S(1)}, u32[]{:S(2)}, u32[]{:S(2)}) %all-to-all-start) | async-done | bytes 98336 | tf_op jit(solution)/shard_map/all_to_all | solution.py:66
  21.2 0.1 fusion.21
  21.3 0.3 fusion
  21.6 0.7 copy.37
  22.4 0.3 copy.40
  22.7 0.3 copy.42
  23.0 0.4 copy-done.4
  23.4 0.6 copy-done.3
  24.1 0.6 copy-done.5
  24.7 0.7 copy.49
  25.5 33.2 %all-gather.3.cloned.1.call-done = bf16[32,128,128]{2,1,0:T(8,128)(2,1)} async-done(((bf16[2,128,128]{2,1,0:T(8,128)(2,1)}), bf16[32,128,128]{2,1,0:T(8,128)(2,1)}) %all-gather.3.cloned.1.call-update) | async-done | bytes 1048592 | tf_op jit(solution)/shard_map/all_gather | solution.py:71
  58.7 2.9 %gather_fusion.1 = bf16[16,2,128,128]{3,2,1,0:T(8,128)(2,1)} fusion(bf16[16,2,128,128]{3,2,1,0:T(8,128)(2,1)} %bitcast.124, s32[1024]{0:T(1024)S(1)} %pad_clamp_fusion), kind=kCustom, calls=%fused_computation.1 | custom fusion | bytes 2097216 | tf_op jit(solution)/shard_map/while/body/eval_jaxpr/gather | solution.py:77
  61.6 2.0 %gather_fusion = bf16[16,2,128,128]{3,2,1,0:T(8,128)(2,1)S(1)} fusion(bf16[16,2,128,128]{3,2,1,0:T(8,128)(2,1)} %bitcast.125, s32[1024]{0:T(1024)S(1)} %pad_clamp_fusion.1), kind=kCustom, calls=%fused_computation | custom fusion | bytes 2097216 | tf_op jit(solution)/shard_map/while/body/eval_jaxpr/gather | solution.py:77
  63.6 1.5 %fusion.5 = f32[16,128,128]{2,1,0:T(8,128)S(1)} fusion(bf16[16,2,128,128]{3,2,1,0:T(8,128)(2,1)} %gather_fusion.1, pred[16]{0:T(512)(128)(4,1)S(1)} %broadcast_compare_fusion, bf16[16,128,128]{1,2,0:T(8,128)(2,1)S(1)} %copy.42, bf16[16,2,128,128]{3,2,1,0:T(8,128)(2,1)S(1)} %copy-done), kind=kOutput, calls=%fused_computation.24 | convolution fusion | flops 67633152 | bytes 2621952 | tf_op jit(solution)/shard_map/while/body/eval_jaxpr/bij,bjk->bik/dot_general | solution.py:31
  65.1 0.4 fusion.3
  65.5 0.8 %copy-done.1 = bf16[16,2,128,128]{3,2,1,0:T(8,128)(2,1)S(1)} copy-done((bf16[16,2,128,128]{3,2,1,0:T(8,128)(2,1)S(1)}, bf16[16,2,128,128]{3,2,1,0:T(8,128)(2,1)}, u32[]{:S(2)}) %copy-start.1) | copy-done | bytes 1048600
  66.3 0.4 fusion.6
  66.7 0.4 fusion.4
  67.1 0.4 convolution_add_fusion
  67.5 0.4 convolution_subtract_fusion
  68.0 0.4 convolution_subtract_fusion.1
  68.4 0.7 subtract_reduce_fusion
  69.1 0.6 pad_maximum_fusion
  (20 shorter events, 0.4 us)
Async XLA Ops:
  7.2 7.5 %copy-start.2 = (s32[64]{0:T(128)S(1)}, s32[64]{0:T(128)}, u32[]{:S(2)}) copy-start(s32[64]{0:T(128)} %param.7) | copy-start | bytes 772
  7.2 15.2 %copy-start = (bf16[16,2,128,128]{3,2,1,0:T(8,128)(2,1)S(1)}, bf16[16,2,128,128]{3,2,1,0:T(8,128)(2,1)}, u32[]{:S(2)}) copy-start(bf16[16,2,128,128]{3,2,1,0:T(8,128)(2,1)} %param.8) | copy-start | bytes 3145732
  7.2 13.9 %all-to-all-start = ((bf16[16,4,2,3,128]{4,2,3,1,0:T(2,128)(2,1)}), bf16[16,4,2,3,128]{4,2,3,1,0:T(2,128)(2,1)S(1)}, u32[]{:S(2)}, u32[]{:S(2)}) async-start(bf16[16,4,2,3,128]{4,2,3,1,0:T(2,128)(2,1)} %param.6), calls=%async_computation | async-start | bytes 196608 | tf_op jit(solution)/shard_map/all_to_all | solution.py:66
  14.7 44.0 %all-gather.3.cloned.1.call-start = ((), (), s32[]{:S(2)}) async-start(), calls=%async_computation.1 | async-start | bytes 1114112 | tf_op jit(solution)/shard_map/all_gather | solution.py:71
  22.7 0.7 copy-start.4
  23.4 0.7 copy-start.3
  24.1 0.7 copy-start.5
  65.1 1.2 %copy-start.1 = (bf16[16,2,128,128]{3,2,1,0:T(8,128)(2,1)S(1)}, bf16[16,2,128,128]{3,2,1,0:T(8,128)(2,1)}, u32[]{:S(2)}) copy-start(bf16[16,2,128,128]{3,2,1,0:T(8,128)(2,1)} %gather_fusion.1) | copy-start | bytes 3145732
Sparse Core Ops, SparseCore 0:
  22.5 36.1 all-gather.2
where the time goes:
time: 77.1 us; the launch traced here: 76.5 us
  waiting for transfers between devices  39.5 us (51%)
  between operations  14.2 us (18%)
  local copies, waits for them, and re-layouts  9.55 us (12%)
  starting transfers between devices  7.52 us (10%)
  matrix products  4.81 us (6%)
  other arithmetic  0.85 us (1%)
    all_gather x1, waiting for transfers between devices, local(): gathered = lax.all_gather(elemental, 'space', axis=0, tiled=True)  33.2 us
    all_to_all x1, starting transfers between devices, local(): lax.all_to_all(eigvecs, 'space', split_axis=0, concat_axis=1, tiled=True)  7.48 us
    all_to_all x1, waiting for transfers between devices, local(): lax.all_to_all(eigvecs, 'space', split_axis=0, concat_axis=1, tiled=True)  6.29 us
    dot_general x8, matrix products, mult(): jnp.einsum('bij,bjk->bik', left, right, preferred_element_type=jnp.float32)  4.56 us
    unnamed x13, local copies, waits for them, and re-layouts  3.24 us
    gather x1, local copies, waits for them, and re-layouts, holder_block(): gathered[source_ids]  2.92 us
    gather x1, local copies, waits for them, and re-layouts, holder_block(): gathered[sink_ids]  1.97 us
  transfers between devices with their start and end apart: 2, of which 2 were waited for; matrix products, arithmetic and copies ran while one was open for 2% of the time, Pallas kernels for 0%

commit v1 on v0

--- a/solution.py
+++ b/solution.py
@@ -1,8 +1,11 @@
+import functools
 import math
 
 import jax
 import jax.numpy as jnp
 from jax import lax
+from jax.experimental import pallas as pl
+from jax.experimental.pallas import tpu as pltpu
 from jax.sharding import PartitionSpec as P
 
 PERIOD = 48
@@ -59,7 +62,7 @@
     return result.reshape((total,) + result.shape[2:])
 
 
-def local(eigvecs, phase_index, perambulator, tile_sink, tile_sep, tile_diagram):
+def local_large(eigvecs, phase_index, perambulator, tile_sink, tile_sep, tile_diagram):
     tile_count = perambulator.shape[0]
     sinks = tile_sink[:, 0]
     cosine, sine = phases(phase_index)
@@ -80,18 +83,353 @@
     return (elemental, correlator)
 
 
+CHUNKS = 2
+VMEM_BLOCKS = 8 * 1024 * 1024
+
+
+def factors(count):
+    chips = count // 2
+    inner = 1
+    while inner * inner * 4 <= chips:
+        inner *= 2
+    while chips % inner:
+        inner //= 2
+    return (chips // inner, inner)
+
+
+def fits(mesh, eigvecs):
+    count = mesh.shape["space"]
+    outer, inner = factors(count)
+    total = eigvecs.size * eigvecs.dtype.itemsize // mesh.shape["groups"]
+    return count % 2 == 0 and inner == 2 and outer >= 2 and total <= VMEM_BLOCKS
+
+
+def kernel(
+    dims,
+    eig_ref,
+    phase_ref,
+    tiles_ref,
+    sink_ref,
+    sep_ref,
+    diag_ref,
+    elem_ref,
+    corr_ref,
+    held,
+    left,
+    right,
+    cos_rows,
+    sin_rows,
+    mats,
+    tile_mats,
+    rows_re,
+    rows_im,
+    send_sem,
+    recv_sem,
+    tile_sem,
+    own_sem,
+):
+    outer, inner, times, rows, nvec, tile_count = dims
+    me = lax.axis_index("space")
+    core = lax.rem(me, 2)
+    chip = lax.div(me, 2)
+    near = lax.rem(chip, inner)
+    far = lax.div(chip, inner)
+    sites = phase_ref.shape[1]
+    per_site = rows // (sites // (outer * inner * 2))
+    groups = rows // 8
+    part = times // CHUNKS * groups
+    pair = 2 * rows
+
+    def index(far_pos, near_pos, core_pos):
+        return (far_pos * inner + near_pos) * 2 + core_pos
+
+    sibling = index(far, near, 1 - core)
+    beside = index(far, 1 - near, core)
+    above = index(far + 1, near, core)
+    below = index(far - 1, near, core)
+    has_above = far < outer - 1
+    has_below = far > 0
+
+    def tile_copies():
+        full = slice(0, nvec)
+        rest = slice(nvec, 2 * nvec)
+        return [
+            pltpu.make_async_copy(tiles_ref.at[:, 0], tile_mats.at[:, full, full], tile_sem.at[0]),
+            pltpu.make_async_copy(tiles_ref.at[:, 1], tile_mats.at[:, full, rest], tile_sem.at[1]),
+            pltpu.make_async_copy(tiles_ref.at[:, 0], tile_mats.at[:, rest, rest], tile_sem.at[2]),
+        ]
+
+    own_copy = pltpu.make_async_copy(eig_ref, held.at[me], own_sem)
+    own_copy.start()
+    for copy in tile_copies():
+        copy.start()
+
+    barrier = pltpu.get_barrier_semaphore()
+
+    def greet(target):
+        pl.semaphore_signal(barrier, inc=1, device_id={"space": target}, device_id_type=pl.DeviceIdType.MESH)
+
+    greet(sibling)
+    greet(beside)
+
+    @pl.when(has_above)
+    def _():
+        greet(above)
+
+    @pl.when(has_below)
+    def _():
+        greet(below)
+
+    pl.semaphore_wait(barrier, 2 + has_above.astype(jnp.int32) + has_below.astype(jnp.int32))
+
+    def piece(ref, chunk):
+        return ref.at[pl.ds(chunk * part, part)]
+
+    def remote(way, target, origin, chunk, own=False):
+        return pltpu.make_async_remote_copy(
+            src_ref=piece(eig_ref, chunk) if own else piece(held.at[origin], chunk),
+            dst_ref=piece(held.at[origin], chunk),
+            send_sem=send_sem.at[way, origin, chunk],
+            recv_sem=recv_sem.at[origin, chunk],
+            device_id={"space": target},
+            device_id_type=pl.DeviceIdType.MESH,
+        )
+
+    def arrived(origin, chunk):
+        remote(0, sibling, origin, chunk).wait_recv()
+
+    for chunk in range(CHUNKS):
+        @pl.when(has_above)
+        def _():
+            remote(2, above, me, chunk, own=True).start()
+
+        @pl.when(has_below)
+        def _():
+            remote(3, below, me, chunk, own=True).start()
+
+        remote(1, beside, me, chunk, own=True).start()
+        remote(0, sibling, me, chunk, own=True).start()
+
+    angle = 2.0 * math.pi / PERIOD * phase_ref[...].astype(jnp.float32)
+    total_rows = sites * per_site
+    row_id = lax.broadcasted_iota(jnp.int32, (total_rows, sites), 0)
+    first_row = lax.broadcasted_iota(jnp.int32, (total_rows, sites), 1) * per_site
+    chosen = (row_id >= first_row) & (row_id < first_row + per_site)
+
+    def spread(values):
+        column = jnp.sum(jnp.where(chosen, values, 0.0), axis=1, keepdims=True)
+        return jnp.broadcast_to(column, (total_rows, nvec))
+
+    cos_rows[...] = spread(jnp.cos(angle))
+    sin_rows[...] = spread(jnp.sin(angle))
+    own_copy.wait()
+
+    def line_step(dist):
+        def upward(start):
+            for chunk in range(CHUNKS):
+                origin = index(far - dist, near, core)
+                if start:
+                    arrived(origin, chunk)
+
+                    @pl.when(has_above)
+                    def _():
+                        remote(2, above, origin, chunk).start()
+
+                    remote(1, beside, origin, chunk).start()
+                    remote(0, sibling, origin, chunk).start()
+
+        def downward(start):
+            for chunk in range(CHUNKS):
+                origin = index(far + dist, near, core)
+                arrived(origin, chunk)
+
+                @pl.when(has_below)
+                def _():
+                    remote(3, below, origin, chunk).start()
+
+                remote(1, beside, origin, chunk).start()
+                remote(0, sibling, origin, chunk).start()
+
+        pl.when(far >= dist)(lambda: upward(True))
+        pl.when(far + dist < outer)(lambda: downward(True))
+
+    def beside_step(dist):
+        def take(far_pos):
+            for chunk in range(CHUNKS):
+                origin = index(far_pos, 1 - near, core)
+                arrived(origin, chunk)
+                remote(0, sibling, origin, chunk).start()
+
+        if dist == 0:
+            take(far)
+        else:
+            pl.when(far >= dist)(lambda: take(far - dist))
+            pl.when(far + dist < outer)(lambda: take(far + dist))
+
+    even = lax.rem(lax.broadcasted_iota(jnp.int32, (pair, nvec), 0), 2) == 0
+
+    def process(far_pos, near_pos):
+        place = far_pos * inner + near_pos
+        other = index(far_pos, near_pos, 1 - core)
+        for chunk in range(CHUNKS):
+            arrived(other, chunk)
+        base = pl.multiple_of(place * pair, pair)
+        cosine = cos_rows[pl.ds(base, pair), :]
+        sine = sin_rows[pl.ds(base, pair), :]
+
+        def one(time, carry):
+            halves = [
+                held[place * 2 + half, pl.ds(time * groups, groups)].astype(jnp.float32).reshape(rows, nvec)
+                for half in range(2)
+            ]
+            vecs = jnp.concatenate(halves, axis=0)
+            swapped = jnp.where(even, pltpu.roll(vecs, pair - 1, 0), -pltpu.roll(vecs, 1, 0))
+            left[time, pl.ds(base, pair), :] = vecs.astype(jnp.bfloat16)
+            right[time, pl.ds(base, pair), 0:nvec] = (cosine * vecs - sine * swapped).astype(jnp.bfloat16)
+            right[time, pl.ds(base, pair), nvec:] = (sine * vecs + cosine * swapped).astype(jnp.bfloat16)
+            return carry
+
+        lax.fori_loop(0, times, one, 0, unroll=4)
+
+    def process_at(dist, near_pos):
+        if dist == 0:
+            process(far, near_pos)
+        else:
+            pl.when(far >= dist)(lambda: process(far - dist, near_pos))
+            pl.when(far + dist < outer)(lambda: process(far + dist, near_pos))
+
+    process_at(0, near)
+    line_step(1)
+    beside_step(0)
+    process_at(1, near)
+    process_at(0, 1 - near)
+    for dist in range(2, outer + 1):
+        if dist < outer:
+            line_step(dist)
+        if dist == 2:
+            for copy in tile_copies():
+                copy.wait()
+            tile_mats[:, nvec:, 0:nvec] = -tile_mats[:, 0:nvec, nvec:]
+        beside_step(dist - 1)
+        if dist < outer:
+            process_at(dist, near)
+        process_at(dist - 1, 1 - near)
+
+    for time in range(times):
+        value = lax.dot_general(
+            left[time], right[time], (((0,), (0,)), ((), ())), preferred_element_type=jnp.float32
+        )
+        real_part = value[:, 0:nvec].astype(jnp.bfloat16)
+        imag_part = value[:, nvec:].astype(jnp.bfloat16)
+        mats[time, 0:nvec, 0:nvec] = real_part
+        mats[time, 0:nvec, nvec:] = imag_part
+        mats[time, nvec:, 0:nvec] = -imag_part
+        mats[time, nvec:, nvec:] = real_part
+
+    elem_ref[0, 0] = mats[me, 0:nvec, 0:nvec]
+    elem_ref[0, 1] = mats[me, 0:nvec, nvec:]
+
+    for tile in range(tile_count):
+        sink = sink_ref[0, tile]
+        source = lax.rem(sink - sep_ref[tile] + times, times)
+        flag = diag_ref[tile] == 1
+        first = jnp.where(flag, source, sink)
+        second = jnp.where(flag, sink, source)
+        ahead = jnp.dot(mats[first, 0:nvec, :], tile_mats[tile], preferred_element_type=jnp.float32)
+        behind = jnp.dot(tile_mats[tile, 0:nvec, :], mats[second], preferred_element_type=jnp.float32)
+        a_re, a_im = ahead[:, 0:nvec], ahead[:, nvec:]
+        b_re, b_im = behind[:, 0:nvec], behind[:, nvec:]
+        sign = jnp.where(flag, -1.0, 1.0)
+        rows_re[tile : tile + 1, :] = jnp.sum(a_re * b_re + a_im * b_im, axis=0, keepdims=True)
+        rows_im[tile : tile + 1, :] = sign * jnp.sum(a_im * b_re - a_re * b_im, axis=0, keepdims=True)
+
+    corr_ref[:, 0:1] = jnp.sum(rows_re[...], axis=1, keepdims=True)
+    corr_ref[:, 1:2] = jnp.sum(rows_im[...], axis=1, keepdims=True)
+
+    def sent(way, origin):
+        for chunk in range(CHUNKS):
+            remote(way, sibling, origin, chunk).wait_send()
+
+    sent(1, me)
+    sent(0, me)
+    pl.when(has_above)(lambda: sent(2, me))
+    pl.when(has_below)(lambda: sent(3, me))
+    sent(0, index(far, 1 - near, core))
+    for dist in range(1, outer):
+        @pl.when(far >= dist)
+        def _():
+            origin = index(far - dist, near, core)
+            sent(0, origin)
+            sent(1, origin)
+            pl.when(has_above)(lambda: sent(2, origin))
+            sent(0, index(far - dist, 1 - near, core))
+
+        @pl.when(far + dist < outer)
+        def _():
+            origin = index(far + dist, near, core)
+            sent(0, origin)
+            sent(1, origin)
+            pl.when(has_below)(lambda: sent(3, origin))
+            sent(0, index(far + dist, 1 - near, core))
+
+
+def local_small(count, eigvecs, phase_index, perambulator, tile_sink, tile_sep, tile_diagram):
+    times, sites, parts, colors, nvec = eigvecs.shape
+    rows = sites * parts * colors
+    tile_count = perambulator.shape[0]
+    outer, inner = factors(count)
+    flat = jnp.transpose(eigvecs, (0, 1, 3, 2, 4)).reshape(times * rows // 8, 8, nvec)
+    vmem = pl.BlockSpec(memory_space=pltpu.VMEM)
+    smem = pl.BlockSpec(memory_space=pltpu.SMEM)
+    hbm = pl.BlockSpec(memory_space=pl.ANY)
+    depth = count * rows
+    return pl.pallas_call(
+        functools.partial(kernel, (outer, inner, times, rows, nvec, tile_count)),
+        out_shape=(
+            jax.ShapeDtypeStruct((1, 2, nvec, nvec), jnp.bfloat16),
+            jax.ShapeDtypeStruct((tile_count, 2), jnp.float32),
+        ),
+        in_specs=[vmem, vmem, hbm, smem, smem, smem],
+        out_specs=(vmem, vmem),
+        scratch_shapes=[
+            pltpu.VMEM((count, times * rows // 8, 8, nvec), jnp.bfloat16),
+            pltpu.VMEM((times, depth, nvec), jnp.bfloat16),
+            pltpu.VMEM((times, depth, 2 * nvec), jnp.bfloat16),
+            pltpu.VMEM((depth, nvec), jnp.float32),
+            pltpu.VMEM((depth, nvec), jnp.float32),
+            pltpu.VMEM((times, 2 * nvec, 2 * nvec), jnp.bfloat16),
+            pltpu.VMEM((tile_count, 2 * nvec, 2 * nvec), jnp.bfloat16),
+            pltpu.VMEM((tile_count, nvec), jnp.float32),
+            pltpu.VMEM((tile_count, nvec), jnp.float32),
+            pltpu.SemaphoreType.DMA((4, count, CHUNKS)),
+            pltpu.SemaphoreType.DMA((count, CHUNKS)),
+            pltpu.SemaphoreType.DMA((3,)),
+            pltpu.SemaphoreType.DMA,
+        ],
+        compiler_params=pltpu.CompilerParams(collective_id=0, has_side_effects=True),
+    )(flat, phase_index.reshape(1, -1), perambulator, tile_sink.reshape(1, -1), tile_sep, tile_diagram)
+
+
 def solution(mesh):
-    return jax.shard_map(
-        local,
-        mesh=mesh,
-        in_specs=(
-            P("groups", "space", None, None, None),
-            P("groups"),
-            P(("groups", "space"), None, None, None),
-            P(("groups", "space"), None),
-            P(("groups", "space")),
-            P(("groups", "space")),
-        ),
-        out_specs=(P(("groups", "space"), None, None, None), P(("groups", "space"), None)),
-        check_vma=False,
-    )
+    def program(*operands):
+        if fits(mesh, operands[0]):
+            body = functools.partial(local_small, mesh.shape["space"])
+        else:
+            body = local_large
+        mapped = jax.shard_map(
+            body,
+            mesh=mesh,
+            in_specs=(
+                P("groups", "space", None, None, None),
+                P("groups"),
+                P(("groups", "space"), None, None, None),
+                P(("groups", "space"), None),
+                P(("groups", "space")),
+                P(("groups", "space")),
+            ),
+            out_specs=(P(("groups", "space"), None, None, None), P(("groups", "space"), None)),
+            check_vma=False,
+        )
+        return mapped(*operands)
+
+    return program

time: 77.1 us -> 27.2 us (0.35)
  waiting for transfers between devices: 39.5 us -> 0 us
  Pallas kernels: 0 us -> 23.5 us
  between operations: 14.2 us -> 0.64 us
  starting transfers between devices: 7.52 us -> 0 us
  local copies, waits for them, and re-layouts: 9.55 us -> 2.81 us
  matrix products: 4.81 us -> 0 us
  other arithmetic: 0.85 us -> 0 us
    all_gather x1 -> x0, waiting for transfers between devices: 33.2 us -> none  [local(): gathered = lax.all_gather(elemental, 'space', axis=0, tiled=True)]
    pallas_call x0 -> x1, Pallas kernels: none -> 23.5 us  [local_small(): pl.pallas_call(functools.partial(kernel, (outer, inner, times, rows, nvec...]
    all_to_all x1 -> x0, starting transfers between devices: 7.48 us -> none  [local(): lax.all_to_all(eigvecs, 'space', split_axis=0, concat_axis=1, tiled=True)]
    all_to_all x1 -> x0, waiting for transfers between devices: 6.29 us -> none  [local(): lax.all_to_all(eigvecs, 'space', split_axis=0, concat_axis=1, tiled=True)]
    gather x2 -> x0, local copies, waits for them, and re-layouts: 4.89 us -> none  [the longest x1 2.92 us: holder_block(): gathered[source_ids]]
    dot_general x9 -> x0, matrix products: 4.81 us -> none  [the longest x8 4.56 us: mult(): jnp.einsum('bij,bjk->bik', left, right, preferred_element_type=jnp.float32)]
    unnamed x13 -> x1, local copies, waits for them, and re-layouts: 3.24 us -> 1.47 us
    pallas_call x0 -> x1, local copies, waits for them, and re-layouts: none -> 1.33 us  [local_small(): pl.pallas_call(functools.partial(kernel, (outer, inner, times, rows, nvec...]
  transfers between devices with their start and end apart: 2 -> 0, of which waited for: 2 -> 0; matrix products, arithmetic and copies ran while one was open for 2% -> 0% of each run, Pallas kernels for 0% -> 0%
where the time goes in v1:
time: 27.2 us; the launch traced here: 27 us
  Pallas kernels  23.5 us (86%)
  local copies, waits for them, and re-layouts  2.81 us (10%)
  between operations  0.64 us (2%)
    pallas_call x1, Pallas kernels, local_small(): pl.pallas_call(functools.partial(kernel, (outer, inner, times, rows, nvec...  23.5 us
    unnamed x1, local copies, waits for them, and re-layouts  1.47 us
    pallas_call x1, local copies, waits for them, and re-layouts, local_small(): pl.pallas_call(functools.partial(kernel, (outer, inner, times, rows, nvec...  1.33 us

profile of v1, /device:TPU:1, one launch (start us, length us, event | category | flops | bytes accessed | tf_op | source)
XLA Modules:
  0.0 27.0 jit_solution(17196280520451170585)
XLA Ops:
  0.6 23.5 %shard_map.77 = (bf16[1,2,128,128]{3,2,1,0:T(8,128)(2,1)}, f32[16,2]{1,0:T(8,128)}) custom-call(bf16[48,8,128]{2,1,0:T(8,128)(2,1)} %bitcast.5, s32[1,64]{1,0:T(1,128)} %bitcast.6, bf16[16,2,128,128]{3,2,1,0:T(8,128)(2,1)} %tiles_ref.1, s32[1,16]{1,0:T(1,128)} %bitcast.7, s32[16]{0:T(128)} %sep_ref.1, s32[16]{0:T(128)} %diag_ref.1), custom_call_target="tpu_custom_call" | custom-call | tf_op jit(solution)/shard_map/pallas_call | solution.py:386
  24.1 1.3 %copy.8 = f32[16,2]{0,1:T(2,128)} copy(f32[16,2]{1,0:T(8,128)} %get-tuple-element.3) | data formatting | bytes 256 | tf_op jit(solution)/shard_map/pallas_call | solution.py:386
  25.5 1.5 %copy.10 = bf16[1,2,128,128]{3,2,1,0:T(8,128)(2,1)} copy(bf16[1,2,128,128]{3,2,1,0:T(8,128)(2,1)} %get-tuple-element.6) | data formatting | bytes 131072

commit v2 on v1

--- a/solution.py
+++ b/solution.py
@@ -83,7 +83,7 @@
     return (elemental, correlator)
 
 
-CHUNKS = 2
+CHUNKS = 1
 VMEM_BLOCKS = 8 * 1024 * 1024
 
 
@@ -107,28 +107,20 @@
 def kernel(
     dims,
     eig_ref,
-    phase_ref,
-    tiles_ref,
-    sink_ref,
-    sep_ref,
-    diag_ref,
-    elem_ref,
-    corr_ref,
+    phase_hbm,
+    mats,
     held,
     left,
     right,
     cos_rows,
     sin_rows,
-    mats,
-    tile_mats,
-    rows_re,
-    rows_im,
     send_sem,
     recv_sem,
-    tile_sem,
     own_sem,
+    phase_ref,
+    phase_sem,
 ):
-    outer, inner, times, rows, nvec, tile_count = dims
+    outer, inner, times, rows, nvec = dims
     me = lax.axis_index("space")
     core = lax.rem(me, 2)
     chip = lax.div(me, 2)
@@ -150,19 +142,10 @@
     has_above = far < outer - 1
     has_below = far > 0
 
-    def tile_copies():
-        full = slice(0, nvec)
-        rest = slice(nvec, 2 * nvec)
-        return [
-            pltpu.make_async_copy(tiles_ref.at[:, 0], tile_mats.at[:, full, full], tile_sem.at[0]),
-            pltpu.make_async_copy(tiles_ref.at[:, 1], tile_mats.at[:, full, rest], tile_sem.at[1]),
-            pltpu.make_async_copy(tiles_ref.at[:, 0], tile_mats.at[:, rest, rest], tile_sem.at[2]),
-        ]
-
     own_copy = pltpu.make_async_copy(eig_ref, held.at[me], own_sem)
     own_copy.start()
-    for copy in tile_copies():
-        copy.start()
+    phase_copy = pltpu.make_async_copy(phase_hbm, phase_ref, phase_sem)
+    phase_copy.start()
 
     barrier = pltpu.get_barrier_semaphore()
 
@@ -210,6 +193,7 @@
         remote(1, beside, me, chunk, own=True).start()
         remote(0, sibling, me, chunk, own=True).start()
 
+    phase_copy.wait()
     angle = 2.0 * math.pi / PERIOD * phase_ref[...].astype(jnp.float32)
     total_rows = sites * per_site
     row_id = lax.broadcasted_iota(jnp.int32, (total_rows, sites), 0)
@@ -306,10 +290,6 @@
     for dist in range(2, outer + 1):
         if dist < outer:
             line_step(dist)
-        if dist == 2:
-            for copy in tile_copies():
-                copy.wait()
-            tile_mats[:, nvec:, 0:nvec] = -tile_mats[:, 0:nvec, nvec:]
         beside_step(dist - 1)
         if dist < outer:
             process_at(dist, near)
@@ -325,26 +305,6 @@
         mats[time, 0:nvec, nvec:] = imag_part
         mats[time, nvec:, 0:nvec] = -imag_part
         mats[time, nvec:, nvec:] = real_part
-
-    elem_ref[0, 0] = mats[me, 0:nvec, 0:nvec]
-    elem_ref[0, 1] = mats[me, 0:nvec, nvec:]
-
-    for tile in range(tile_count):
-        sink = sink_ref[0, tile]
-        source = lax.rem(sink - sep_ref[tile] + times, times)
-        flag = diag_ref[tile] == 1
-        first = jnp.where(flag, source, sink)
-        second = jnp.where(flag, sink, source)
-        ahead = jnp.dot(mats[first, 0:nvec, :], tile_mats[tile], preferred_element_type=jnp.float32)
-        behind = jnp.dot(tile_mats[tile, 0:nvec, :], mats[second], preferred_element_type=jnp.float32)
-        a_re, a_im = ahead[:, 0:nvec], ahead[:, nvec:]
-        b_re, b_im = behind[:, 0:nvec], behind[:, nvec:]
-        sign = jnp.where(flag, -1.0, 1.0)
-        rows_re[tile : tile + 1, :] = jnp.sum(a_re * b_re + a_im * b_im, axis=0, keepdims=True)
-        rows_im[tile : tile + 1, :] = sign * jnp.sum(a_im * b_re - a_re * b_im, axis=0, keepdims=True)
-
-    corr_ref[:, 0:1] = jnp.sum(rows_re[...], axis=1, keepdims=True)
-    corr_ref[:, 1:2] = jnp.sum(rows_im[...], axis=1, keepdims=True)
 
     def sent(way, origin):
         for chunk in range(CHUNKS):
@@ -373,6 +333,33 @@
             sent(0, index(far + dist, 1 - near, core))
 
 
+def contract_kernel(mats, tiles_ref, sink_ref, sep_ref, diag_ref, elem_ref, corr_ref, rows_re, rows_im):
+    me = lax.axis_index("space")
+    times = mats.shape[0]
+    tile_count, _, nvec, _ = tiles_ref.shape
+    elem_ref[0, 0] = mats[me, 0:nvec, 0:nvec]
+    elem_ref[0, 1] = mats[me, 0:nvec, nvec:]
+
+    for tile in range(tile_count):
+        sink = sink_ref[0, tile]
+        source = lax.rem(sink - sep_ref[tile] + times, times)
+        flag = diag_ref[tile] == 1
+        first = jnp.where(flag, source, sink)
+        second = jnp.where(flag, sink, source)
+        top = jnp.concatenate([tiles_ref[tile, 0], tiles_ref[tile, 1]], axis=1)
+        both = jnp.concatenate([top, jnp.concatenate([-tiles_ref[tile, 1], tiles_ref[tile, 0]], axis=1)], axis=0)
+        ahead = jnp.dot(mats[first, 0:nvec, :], both, preferred_element_type=jnp.float32)
+        behind = jnp.dot(top, mats[second], preferred_element_type=jnp.float32)
+        a_re, a_im = ahead[:, 0:nvec], ahead[:, nvec:]
+        b_re, b_im = behind[:, 0:nvec], behind[:, nvec:]
+        sign = jnp.where(flag, -1.0, 1.0)
+        rows_re[tile : tile + 1, :] = jnp.sum(a_re * b_re + a_im * b_im, axis=0, keepdims=True)
+        rows_im[tile : tile + 1, :] = sign * jnp.sum(a_im * b_re - a_re * b_im, axis=0, keepdims=True)
+
+    corr_ref[0] = jnp.sum(rows_re[...], axis=1)
+    corr_ref[1] = jnp.sum(rows_im[...], axis=1)
+
+
 def local_small(count, eigvecs, phase_index, perambulator, tile_sink, tile_sep, tile_diagram):
     times, sites, parts, colors, nvec = eigvecs.shape
     rows = sites * parts * colors
@@ -380,34 +367,45 @@
     outer, inner = factors(count)
     flat = jnp.transpose(eigvecs, (0, 1, 3, 2, 4)).reshape(times * rows // 8, 8, nvec)
     vmem = pl.BlockSpec(memory_space=pltpu.VMEM)
+    hbm = pl.BlockSpec(memory_space=pltpu.HBM)
     smem = pl.BlockSpec(memory_space=pltpu.SMEM)
-    hbm = pl.BlockSpec(memory_space=pl.ANY)
     depth = count * rows
-    return pl.pallas_call(
-        functools.partial(kernel, (outer, inner, times, rows, nvec, tile_count)),
-        out_shape=(
-            jax.ShapeDtypeStruct((1, 2, nvec, nvec), jnp.bfloat16),
-            jax.ShapeDtypeStruct((tile_count, 2), jnp.float32),
-        ),
-        in_specs=[vmem, vmem, hbm, smem, smem, smem],
-        out_specs=(vmem, vmem),
+    mats = pl.pallas_call(
+        functools.partial(kernel, (outer, inner, times, rows, nvec)),
+        out_shape=jax.ShapeDtypeStruct((times, 2 * nvec, 2 * nvec), jnp.bfloat16),
+        in_specs=[hbm, hbm],
+        out_specs=vmem,
         scratch_shapes=[
             pltpu.VMEM((count, times * rows // 8, 8, nvec), jnp.bfloat16),
             pltpu.VMEM((times, depth, nvec), jnp.bfloat16),
             pltpu.VMEM((times, depth, 2 * nvec), jnp.bfloat16),
             pltpu.VMEM((depth, nvec), jnp.float32),
             pltpu.VMEM((depth, nvec), jnp.float32),
-            pltpu.VMEM((times, 2 * nvec, 2 * nvec), jnp.bfloat16),
-            pltpu.VMEM((tile_count, 2 * nvec, 2 * nvec), jnp.bfloat16),
+            pltpu.SemaphoreType.DMA((4 + 2 * outer, count, CHUNKS)),
+            pltpu.SemaphoreType.DMA((count, CHUNKS)),
+            pltpu.SemaphoreType.DMA,
+            pltpu.VMEM((1, phase_index.shape[0]), jnp.int32),
+            pltpu.SemaphoreType.DMA,
+        ],
+        compiler_params=pltpu.CompilerParams(
+            collective_id=0, has_side_effects=True, vmem_limit_bytes=24 * 1024 * 1024
+        ),
+    )(pltpu.with_memory_space_constraint(flat, pltpu.HBM), pltpu.with_memory_space_constraint(phase_index.reshape(1, -1), pltpu.HBM))
+    elementals, correlator = pl.pallas_call(
+        contract_kernel,
+        out_shape=(
+            jax.ShapeDtypeStruct((1, 2, nvec, nvec), jnp.bfloat16),
+            jax.ShapeDtypeStruct((2, tile_count), jnp.float32),
+        ),
+        in_specs=[vmem, vmem, smem, smem, smem],
+        out_specs=(vmem, vmem),
+        scratch_shapes=[
             pltpu.VMEM((tile_count, nvec), jnp.float32),
             pltpu.VMEM((tile_count, nvec), jnp.float32),
-            pltpu.SemaphoreType.DMA((4, count, CHUNKS)),
-            pltpu.SemaphoreType.DMA((count, CHUNKS)),
-            pltpu.SemaphoreType.DMA((3,)),
-            pltpu.SemaphoreType.DMA,
         ],
-        compiler_params=pltpu.CompilerParams(collective_id=0, has_side_effects=True),
-    )(flat, phase_index.reshape(1, -1), perambulator, tile_sink.reshape(1, -1), tile_sep, tile_diagram)
+        compiler_params=pltpu.CompilerParams(vmem_limit_bytes=24 * 1024 * 1024),
+    )(mats, perambulator, tile_sink.reshape(1, -1), tile_sep, tile_diagram)
+    return (elementals, correlator.T)
 
 
 def solution(mesh):

time: 27.2 us -> 25.7 us (0.945)
  local copies, waits for them, and re-layouts: 2.81 us -> 0.02 us
  Pallas kernels: 23.5 us -> 24.9 us
    pallas_call x0 -> x1, Pallas kernels: none -> 1.93 us  [local_small(): pl.pallas_call(contract_kernel, out_shape=(jax.ShapeDtypeStruct((1, 2, nv...]
    unnamed x1 -> x8, local copies, waits for them, and re-layouts: 1.47 us -> 0.02 us
    pallas_call x1 -> x0, local copies, waits for them, and re-layouts: 1.33 us -> none  [local_small(): pl.pallas_call(functools.partial(kernel, (outer, inner, times, rows, nvec...]
    pallas_call x1, Pallas kernels: 23.5 us -> 22.9 us  [local_small(): pl.pallas_call(functools.partial(kernel, (outer, inner, times, rows, nvec...]
where the time goes in v2:
time: 25.7 us; the launch traced here: 25.6 us
  Pallas kernels  24.9 us (97%)
  between operations  0.7 us (3%)
    pallas_call x1, Pallas kernels, local_small(): pl.pallas_call(functools.partial(kernel, (outer, inner, times, rows, nvec...  22.9 us
    pallas_call x1, Pallas kernels, local_small(): pl.pallas_call(contract_kernel, out_shape=(jax.ShapeDtypeStruct((1, 2, nv...  1.93 us

profile of v2, /device:TPU:1, one launch (start us, length us, event | category | flops | bytes accessed | tf_op | source)
XLA Modules:
  0.0 25.6 jit_solution(9240722082703265083)
XLA Ops:
  0.6 0.0 copy-start.3
  0.6 0.0 copy-start.2
  0.7 0.0 copy-start.1
  0.7 0.0 copy-start
  0.7 22.9 %shard_map.77.mats = bf16[16,256,256]{2,1,0:T(8,128)(2,1)S(1)} custom-call(bf16[48,8,128]{2,1,0:T(8,128)(2,1)} %bitcast.7, s32[1,64]{1,0:T(1,128)} %bitcast.8), custom_call_target="tpu_custom_call" | custom-call | tf_op jit(solution)/shard_map/pallas_call | solution.py:373
  23.6 0.0 copy-done.3
  23.6 0.0 copy-done.2
  23.6 0.0 copy-done.1
  23.6 0.0 copy-done
  23.6 1.9 %shard_map.78 = (bf16[1,2,128,128]{3,2,1,0:T(8,128)(2,1)}, f32[2,16]{1,0:T(2,128)}) custom-call(bf16[16,256,256]{2,1,0:T(8,128)(2,1)S(1)} %shard_map.77.mats, bf16[16,2,128,128]{3,2,1,0:T(8,128)(2,1)S(1)} %copy-done, s32[1,16]{1,0:T(1,128)S(1)} %bitcast.6, s32[16]{0:T(128)S(1)} %copy-done.2, s32[16]{0:T(128)S(1)} %copy-done.3), custom_call_target="tpu_custom_call" | custom-call | tf_op jit(solution)/shard_map/pallas_call | solution.py:394
Async XLA Ops:
  0.6 23.0 %copy-start.3 = (s32[16]{0:T(128)S(1)}, s32[16]{0:T(128)}, u32[]{:S(2)}) copy-start(s32[16]{0:T(128)} %diag_ref.1) | copy-start | bytes 196
  0.6 23.0 %copy-start.2 = (s32[16]{0:T(128)S(1)}, s32[16]{0:T(128)}, u32[]{:S(2)}) copy-start(s32[16]{0:T(128)} %sep_ref.1) | copy-start | bytes 196
  0.7 23.0 %copy-start.1 = (s32[16,1]{0,1:T(1,128)S(1)}, s32[16,1]{0,1:T(1,128)}, u32[]{:S(2)}) copy-start(s32[16,1]{0,1:T(1,128)} %param.9) | copy-start | bytes 196
  0.7 23.0 %copy-start = (bf16[16,2,128,128]{3,2,1,0:T(8,128)(2,1)S(1)}, bf16[16,2,128,128]{3,2,1,0:T(8,128)(2,1)}, u32[]{:S(2)}) copy-start(bf16[16,2,128,128]{3,2,1,0:T(8,128)(2,1)} %tiles_ref.1) | copy-start | bytes 3145732
